TPU v7x, 1024 devices: a whole 4x8x16 slice. The times are simulated.
1024 devices in a mesh: wide: 64 (over y_lo, z, core), narrow: 16 (over x, y_hi).
Axes of the slice: x: 4, y: 8 (y_hi: 4, y_lo: 2; y = y_hi * 2 + y_lo), z: 16, core: 2. Of those that a mesh axis runs over, the one named last changes fastest.
Arguments:
- state: float32 [2, 134217728], P(None, ('wide', 'narrow')), may hold values from -6 to 6
- gates: float32 [4, 2, 128, 128], replicated, may hold values from -0.375 to 0.375
- phase_index: int32 [3, 128], replicated, may hold values from 0 to 255
Outputs:
- final_state: float32 [2, 134217728], P(None, ('wide', 'narrow'))
All inputs are finite; a program needn't handle non-finite values.
Results may differ from a plain program's by a relative error of at most 0.00007.
Values sent between devices are 32-bit elements; how exact they have to be, the bound alone decides.
No kernel may reach another device: no remote copies, remote signals or barrier semaphores. Data moves between devices by JAX's collectives and lax.ppermute only.
A program may use at most 32 MiB of HBM per device.

v0:
```python
import math

import jax
import jax.numpy as jnp
from jax import lax
from jax.sharding import PartitionSpec as P

GATE = 128


angle_step = 2.0 * math.pi / 256.0


def swapped(value, axis, distance):
    mask = 2**distance
    pairs = [(source, source ^ mask) for source in range(lax.axis_size(axis))]
    return lax.ppermute(value, axis, pairs)


def real_form(gate_re, gate_im):
    upper = jnp.stack([gate_re, -gate_im], axis=1)
    lower = jnp.stack([gate_im, gate_re], axis=1)
    return jnp.stack([upper, lower], axis=0)


def apply_last(blocks, amplitudes):
    return jnp.einsum("pmqn,qrn->prm", blocks, amplitudes, precision=lax.Precision.HIGHEST)


def apply_middle(blocks, amplitudes):
    return jnp.einsum("pmqn,qbnc->pbmc", blocks, amplitudes, precision=lax.Precision.HIGHEST)


def apply_front(blocks, amplitudes):
    return jnp.einsum("pmqn,qnk->pmk", blocks, amplitudes, precision=lax.Precision.HIGHEST)


def rotate(amplitudes, angle_sum):
    angles = angle_sum.astype(jnp.float32) * angle_step
    cosine = jnp.cos(angles)
    sine = jnp.sin(angles)
    real_part = amplitudes[0] * cosine - amplitudes[1] * sine
    imag_part = amplitudes[0] * sine + amplitudes[1] * cosine
    return jnp.stack([real_part, imag_part], axis=0)


def half_swap(amplitudes, wide_bit, top_bit):
    kept_half = lax.dynamic_index_in_dim(amplitudes, wide_bit, 1, keepdims=False)
    sent_half = lax.dynamic_index_in_dim(amplitudes, 1 - wide_bit, 1, keepdims=False)
    received = swapped(sent_half, "wide", top_bit)
    return jnp.where(
        wide_bit == 0,
        jnp.stack([kept_half, received], axis=1),
        jnp.stack([received, kept_half], axis=1),
    )


def local(state, gates, phase_index):
    local_amps = state.shape[1]
    narrow_count = lax.axis_size("narrow")
    wide_count = lax.axis_size("wide")
    top_bit = wide_count.bit_length() - 2
    wide_bit = lax.axis_index("wide") // (wide_count // 2)
    device = lax.axis_index("wide") * narrow_count + lax.axis_index("narrow")
    half_gate = GATE // 2
    row_count = local_amps // GATE
    amps = apply_last(real_form(gates[0, 0], gates[0, 1]), state.reshape(2, row_count, GATE))
    amps = apply_middle(
        real_form(gates[1, 0], gates[1, 1]),
        amps.reshape(2, local_amps // (GATE * GATE), GATE, GATE),
    )
    span_rows = local_amps * wide_count * narrow_count // (GATE * GATE)
    row_ids = device * row_count + lax.iota(jnp.int32, row_count)
    middle_part = jnp.tile(phase_index[1], row_count // GATE)
    top_ids = row_ids // span_rows
    one_hot = top_ids[:, None] == lax.iota(jnp.int32, GATE)[None, :]
    top_part = jnp.sum(jnp.where(one_hot, phase_index[2][None, :], 0), axis=1)
    angle_sum = phase_index[0][None, :] + (middle_part + top_part)[:, None]
    amps = rotate(amps.reshape(2, row_count, GATE), angle_sum)
    third = real_form(gates[2, 0], gates[2, 1])
    fourth = real_form(gates[3, 0], gates[3, 1])
    laid_out = amps.reshape(2, narrow_count, GATE // narrow_count, local_amps // GATE)
    portion = lax.all_to_all(laid_out, "narrow", split_axis=1, concat_axis=1, tiled=True)
    columns = portion.shape[3]
    current = apply_front(third, portion.reshape(2, GATE, columns)).reshape(
        2, 2, half_gate, columns
    )
    current = half_swap(current, wide_bit, top_bit)
    current = apply_front(fourth, current.reshape(2, GATE, columns)).reshape(
        2, 2, half_gate, columns
    )
    current = half_swap(current, wide_bit, top_bit)
    current = current.reshape(2, narrow_count, GATE // narrow_count, columns)
    result = lax.all_to_all(current, "narrow", split_axis=1, concat_axis=1, tiled=True)
    return result.reshape(2, local_amps)


def solution(mesh):
    in_specs = (P(None, ("wide", "narrow")), P(), P())
    out_specs = P(None, ("wide", "narrow"))
    return jax.shard_map(local, mesh=mesh, in_specs=in_specs, out_specs=out_specs, check_vma=False)
```

profile of v0, /device:TPU:768, one launch (start us, length us, event | category | flops | bytes accessed | tf_op | source)
XLA Modules:
  0.0 115.3 jit_solution(11434428683734740916)
XLA Ops:
  0.0 1.2 %slice_bitcast_fusion = (f32[128,1,128]{2,0,1:T(8,128)S(1)}, f32[128,1,128]{2,0,1:T(8,128)S(1)}, f32[128,1,128]{2,0,1:T(8,128)S(1)}, f32[128,1,128]{2,0,1:T(8,12...) fusion(f32[4,2,128,128]{3,2,1,0:T(8,128)} %param.4), kind=kLoop, calls=%fused_computation.38 | loop fusion | bytes 1048576 | tf_op jit(solution)/shard_map/squeeze | solution.py:69
  1.4 0.3 copy-done.1
  1.6 1.1 fusion
  2.7 0.2 copy.46
  2.9 1.0 convolution_bitcast_fusion.2
  4.0 0.2 copy.28
  4.3 0.2 copy.29
  4.7 0.7 copy-done.2
  5.3 0.4 select_reduce_fusion
  5.7 0.2 add.89
  6.0 2.1 %multiply_subtract_fusion = (f32[1,16,8,1024]{3,2,1,0:T(8,128)S(1)}, f32[1,16,8,1024]{3,2,1,0:T(8,128)S(1)}) fusion(f32[1,16,8,1024]{3,2,1,0:T(8,128)S(1)} %squeeze.34, f32[1,16,8,1024]{3,2,1,0:T(8,128)S(1)} %squeeze.33, s32[1,16,8,1024]{3,2,1,0:T(8,128)S(1)} %add.90, s32[1024]{0:T(1024)S(1)} %broadcast_bitcast_fusion), kind=kLoop, calls=%fused_computation.16 | loop fusion | flops 1179648 | bytes 2625536 | tf_op jit(solution)/shard_map/sub | solution.py:42
  8.2 1.1 copy.30
  9.3 9.7 %all-to-all-start = ((f32[2,16,8,1024]{3,2,0,1:T(8,128)}), f32[2,16,8,1024]{3,2,0,1:T(8,128)S(1)}, u32[]{:S(2)}, u32[]{:S(2)}) async-start(f32[2,16,8,1024]{3,2,0,1:T(8,128)} %copy.30), calls=%async_computation | async-start | bytes 2097152 | tf_op jit(solution)/shard_map/all_to_all | solution.py:83
  19.1 29.6 %all-to-all-done = f32[2,16,8,1024]{3,2,0,1:T(8,128)S(1)} async-done(((f32[2,16,8,1024]{3,2,0,1:T(8,128)}), f32[2,16,8,1024]{3,2,0,1:T(8,128)S(1)}, u32[]{:S(2)}, u32[]{:S(2)}) %all-to-all-start) | async-done | bytes 1048608 | tf_op jit(solution)/shard_map/all_to_all | solution.py:83
  48.7 1.0 convolution_bitcast_fusion.1
  49.8 1.9 %collective-permute-start = (f32[2,64,1024]{2,1,0:T(8,128)S(1)}, f32[2,64,1024]{2,1,0:T(8,128)S(1)}, u32[]{:S(2)}, u32[]{:S(2)}) collective-permute-start(f32[2,64,1024]{2,1,0:T(8,128)S(1)} %get-tuple-element.10), channel_id=1, source_target_pairs={{0,512},{16,528},{32,544},{48,560},{64,576},{80,592},{96,608},{112... | collective-permute-start | bytes 1572872 | tf_op jit(solution)/shard_map/ppermute | solution.py:17
  51.8 11.3 %collective-permute-done = f32[2,64,1024]{2,1,0:T(8,128)S(1)} collective-permute-done((f32[2,64,1024]{2,1,0:T(8,128)S(1)}, f32[2,64,1024]{2,1,0:T(8,128)S(1)}, u32[]{:S(2)}, u32[]{:S(2)}) %collective-permute-start) | collective-permute-done | bytes 524320 | tf_op jit(solution)/shard_map/ppermute | solution.py:17
  63.0 0.1 maximum_select_fusion
  63.2 1.0 convolution_bitcast_fusion
  64.3 2.2 %collective-permute-start.1 = (f32[2,64,1024]{2,1,0:T(8,128)S(1)}, f32[2,64,1024]{2,1,0:T(8,128)S(1)}, u32[]{:S(2)}, u32[]{:S(2)}) collective-permute-start(f32[2,64,1024]{2,1,0:T(8,128)S(1)} %get-tuple-element.8), channel_id=1, source_target_pairs={{0,512},{16,528},{32,544},{48,560},{64,576},{80,592},{96,608},{112... | collective-permute-start | bytes 1572872 | tf_op jit(solution)/shard_map/ppermute | solution.py:17
  66.5 10.2 %collective-permute-done.1 = f32[2,64,1024]{2,1,0:T(8,128)S(1)} collective-permute-done((f32[2,64,1024]{2,1,0:T(8,128)S(1)}, f32[2,64,1024]{2,1,0:T(8,128)S(1)}, u32[]{:S(2)}, u32[]{:S(2)}) %collective-permute-start.1) | collective-permute-done | bytes 524320 | tf_op jit(solution)/shard_map/ppermute | solution.py:17
  76.7 0.1 maximum_select_fusion.1
  76.9 36.6 %all_to_all.10 = f32[2,16,8,1024]{3,2,0,1:T(8,128)S(1)} all-to-all(f32[2,16,8,1024]{3,2,0,1:T(8,128)S(1)} %copy.34), channel_id=1, replica_groups=mesh['wide'=64,'narrow'=16] {'narrow'}, dimensions={1} | all-to-all | bytes 2097152 | tf_op jit(solution)/shard_map/all_to_all | solution.py:94
  113.6 1.8 %copy.47 = f32[1,2,128,1024]{3,1,2,0:T(2,128)} copy(f32[1,2,128,1024]{3,2,1,0:T(8,128)S(1)} %bitcast.133) | data formatting | bytes 2097152
  (22 shorter events, 1.0 us)
Async XLA Ops:
  0.0 1.3 %copy-start = (f32[4,2,128,128]{3,2,1,0:T(8,128)S(1)}, f32[4,2,128,128]{3,2,1,0:T(8,128)}, u32[]{:S(2)}) copy-start(f32[4,2,128,128]{3,2,1,0:T(8,128)} %param.4) | copy-start | bytes 1572868
  0.0 1.6 %copy-start.1 = (f32[2,131072]{1,0:T(2,128)S(1)}, f32[2,131072]{1,0:T(2,128)}, u32[]{:S(2)}) copy-start(f32[2,131072]{1,0:T(2,128)} %param.3) | copy-start | bytes 3145732
  4.6 0.7 copy-start.2
  9.3 39.4 %all-to-all-start = ((f32[2,16,8,1024]{3,2,0,1:T(8,128)}), f32[2,16,8,1024]{3,2,0,1:T(8,128)S(1)}, u32[]{:S(2)}, u32[]{:S(2)}) async-start(f32[2,16,8,1024]{3,2,0,1:T(8,128)} %copy.30), calls=%async_computation | async-start | bytes 2097152 | tf_op jit(solution)/shard_map/all_to_all | solution.py:83
  49.8 13.2 %collective-permute-start = (f32[2,64,1024]{2,1,0:T(8,128)S(1)}, f32[2,64,1024]{2,1,0:T(8,128)S(1)}, u32[]{:S(2)}, u32[]{:S(2)}) collective-permute-start(f32[2,64,1024]{2,1,0:T(8,128)S(1)} %get-tuple-element.10), channel_id=1, source_target_pairs={{0,512},{16,528},{32,544},{48,560},{64,576},{80,592},{96,608},{112... | collective-permute-start | bytes 1572872 | tf_op jit(solution)/shard_map/ppermute | solution.py:17
  64.3 12.4 %collective-permute-start.1 = (f32[2,64,1024]{2,1,0:T(8,128)S(1)}, f32[2,64,1024]{2,1,0:T(8,128)S(1)}, u32[]{:S(2)}, u32[]{:S(2)}) collective-permute-start(f32[2,64,1024]{2,1,0:T(8,128)S(1)} %get-tuple-element.8), channel_id=1, source_target_pairs={{0,512},{16,528},{32,544},{48,560},{64,576},{80,592},{96,608},{112... | collective-permute-start | bytes 1572872 | tf_op jit(solution)/shard_map/ppermute | solution.py:17
where the time goes:
time: 116 us; the launch traced here: 115 us
  waiting for transfers between devices  51.1 us (44%)
  blocking collectives  36.6 us (32%)
  starting transfers between devices  13.8 us (12%)
  local copies, waits for them, and re-layouts  6.51 us (6%)
  matrix products  4.17 us (4%)
  other arithmetic  2.92 us (3%)
    all_to_all x1, blocking collectives, local(): lax.all_to_all(current, 'narrow', split_axis=1, concat_axis=1, tiled=True)  36.6 us
    all_to_all x1, waiting for transfers between devices, local(): lax.all_to_all(laid_out, 'narrow', split_axis=1, concat_axis=1, tiled=True)  29.6 us
    ppermute x2, waiting for transfers between devices, swapped(): return lax.ppermute(value, axis, pairs)  21.4 us
    all_to_all x1, starting transfers between devices, local(): lax.all_to_all(laid_out, 'narrow', split_axis=1, concat_axis=1, tiled=True)  9.67 us
    ppermute x2, starting transfers between devices, swapped(): return lax.ppermute(value, axis, pairs)  4.12 us
    unnamed x8, local copies, waits for them, and re-layouts  2.99 us
  transfers between devices with their start and end apart: 3, of which 3 were waited for; matrix products, arithmetic and copies ran while one was open for 0% of the time, Pallas kernels for 0%

commit v1 on v0

v1 whole, which is shorter than its diff:
```python
import math

import jax
import jax.numpy as jnp
from jax import lax
from jax.experimental import pallas as pl
from jax.experimental.pallas import tpu as pltpu
from jax.sharding import Mesh, PartitionSpec as P

GATE = 128
LANES = 128
GROUP = 32

angle_step = 2.0 * math.pi / 256.0


def dot(a, b):
    return jnp.dot(a, b, preferred_element_type=jnp.float32)


def split(value):
    high = value.astype(jnp.bfloat16)
    return high, (value - high.astype(jnp.float32)).astype(jnp.bfloat16)


def product(left, right):
    (left_high, left_low), (right_high, right_low) = left, right
    return dot(left_high, right_high) + (dot(left_high, right_low) + dot(left_low, right_high))


def real_form(gate_re, gate_im):
    upper = jnp.concatenate([gate_re, -gate_im], axis=1)
    lower = jnp.concatenate([gate_im, gate_re], axis=1)
    return jnp.concatenate([upper, lower], axis=0)


def first_kernel(x_ref, gates_ref, phase_ref, phase_smem, out_ref, phase_cols, mat_ref):
    top = lax.axis_index("top") * 64 + lax.axis_index("rest") * 2 + lax.axis_index("narrow") // 8
    top_phase = phase_smem[2, top]
    lane_angle = phase_ref[0:1, :].astype(jnp.float32) * angle_step
    row_angle = (phase_ref[1:2, :] + top_phase).astype(jnp.float32) * angle_step
    lane_cos, lane_sin = jnp.cos(lane_angle), jnp.sin(lane_angle)
    phase_cols[0] = jnp.broadcast_to(jnp.cos(row_angle), (GATE, LANES)).T
    phase_cols[1] = jnp.broadcast_to(jnp.sin(row_angle), (GATE, LANES)).T

    zero_re, zero_im = gates_ref[0, 0].T, gates_ref[0, 1].T
    turned_re = zero_re * lane_cos - zero_im * lane_sin
    turned_im = zero_re * lane_sin + zero_im * lane_cos
    right = split(
        jnp.concatenate(
            [
                jnp.concatenate([turned_re, turned_im], axis=1),
                jnp.concatenate([-turned_im, turned_re], axis=1),
            ],
            axis=0,
        )
    )
    for high in range(2):
        for low in range(8):
            rows = pl.ds(high * 64 + low, 8, stride=8)
            one_re, one_im = gates_ref[1, 0, rows, :], gates_ref[1, 1, rows, :]
            cosine, sine = phase_cols[0, rows, :], phase_cols[1, rows, :]
            turned_re = one_re * cosine - one_im * sine
            turned_im = one_re * sine + one_im * cosine
            at = high * 128 + low * 16
            mat_ref[at : at + 8, :LANES] = turned_re
            mat_ref[at : at + 8, LANES:] = -turned_im
            mat_ref[at + 8 : at + 16, :LANES] = turned_im
            mat_ref[at + 8 : at + 16, LANES:] = turned_re
    left = split(mat_ref[...])

    for pair in range(4):
        base = pair * 4 * GATE
        real = x_ref[pl.ds(base, 2 * GATE, stride=2), :]
        imag = x_ref[pl.ds(base + 1, 2 * GATE, stride=2), :]
        moved = product(split(jnp.concatenate([real, imag], axis=1)), right)
        turned = jnp.concatenate(
            [
                jnp.concatenate([moved[:GATE, :LANES], moved[GATE:, :LANES]], axis=1),
                jnp.concatenate([moved[:GATE, LANES:], moved[GATE:, LANES:]], axis=1),
            ],
            axis=0,
        )
        done = product(left, split(turned))
        for half in range(2):
            block = pair * 2 + half
            out_ref[block * 4 : block * 4 + 4] = done[:, half * LANES : (half + 1) * LANES].reshape(4, 64, LANES)


def second_kernel(x_ref, gates_ref, out_ref):
    third = split(real_form(gates_ref[2, 0], gates_ref[2, 1]))
    fourth = split(real_form(gates_ref[3, 0], gates_ref[3, 1]))
    for quarter in range(4):
        row = quarter * 16

        def part(which, side):
            rows = slice(row + side * 8, row + side * 8 + 8)
            return x_ref[which * 16 : which * 16 + 16, rows, :].reshape(GATE, LANES)

        gathered = jnp.concatenate(
            [jnp.concatenate([part(0, side), part(1, side)], axis=1) for side in range(2)], axis=0
        )
        moved = product(third, split(gathered))

        def piece(side, which, half):
            at = side * GATE + half * 64
            return moved[at : at + 64, which * LANES : (which + 1) * LANES]

        turned = jnp.concatenate(
            [
                jnp.concatenate([piece(side, which, 0), piece(side, which, 1)], axis=1)
                for side in range(2)
                for which in range(2)
            ],
            axis=0,
        )
        done = product(fourth, split(turned))
        for side in range(2):
            for which in range(2):
                for low in range(8):
                    for half in range(2):
                        at = side * 128 + which * 64 + low * 8
                        out_ref[which * 16 + half * 8 + low, pl.ds(quarter * 2 + side, 8, stride=8), :] = done[
                            at : at + 8, half * LANES : (half + 1) * LANES
                        ]


def last_kernel(x_ref, out_ref):
    for bit in range(2):
        out_ref[:, :, bit] = x_ref[:, bit]


def in_vmem():
    return pl.BlockSpec(memory_space=pltpu.VMEM)


def local(state, gates, phase_index):
    local_amps = state.shape[1]
    rows = state.reshape(2, local_amps // LANES, LANES).transpose(1, 0, 2).reshape(2 * local_amps // LANES, LANES)
    chunked = jax.ShapeDtypeStruct((GROUP, 64, LANES), jnp.float32)
    sent = pl.pallas_call(
        first_kernel,
        out_shape=chunked,
        in_specs=[in_vmem(), in_vmem(), in_vmem(), pl.BlockSpec(memory_space=pltpu.SMEM)],
        out_specs=in_vmem(),
        scratch_shapes=[
            pltpu.VMEM((2, GATE, LANES), jnp.float32),
            pltpu.VMEM((2 * GATE, 2 * GATE), jnp.float32),
        ],
    )(rows, gates, phase_index, phase_index)
    group = ("top", "narrow")
    held = lax.all_to_all(sent, group, 0, 0, tiled=True)
    back = pl.pallas_call(
        second_kernel,
        out_shape=chunked,
        in_specs=[in_vmem(), in_vmem()],
        out_specs=in_vmem(),
    )(held, gates)
    home = lax.all_to_all(back, group, 0, 0, tiled=True)
    ordered = pl.pallas_call(
        last_kernel,
        out_shape=jax.ShapeDtypeStruct((16, 8, 2, 8, LANES), jnp.float32),
        in_specs=[in_vmem()],
        out_specs=in_vmem(),
    )(home.reshape(16, 2, 8, 8, LANES))
    return ordered.reshape(local_amps // LANES, 2, LANES).transpose(1, 0, 2).reshape(2, local_amps)


def solution(mesh):
    wide, narrow = mesh.devices.shape
    split_mesh = Mesh(mesh.devices.reshape(2, wide // 2, narrow), ("top", "rest", "narrow"))
    amplitudes = P(None, ("top", "rest", "narrow"))
    return jax.shard_map(
        local, mesh=split_mesh, in_specs=(amplitudes, P(), P()), out_specs=amplitudes, check_vma=False
    )
```

time: 116 us -> 81.2 us (0.70)
  the two profiles are of different devices: /device:TPU:768 before, /device:TPU:896 now
where the time goes in v1:
time: 81.2 us; the launch traced here: 80.8 us
  blocking collectives  71.1 us (88%)
  Pallas kernels  9.67 us (12%)
    all_to_all x1, blocking collectives, local(): held = lax.all_to_all(sent, group, 0, 0, tiled=True)  37.6 us
    all_to_all x1, blocking collectives, local(): home = lax.all_to_all(back, group, 0, 0, tiled=True)  33.5 us
    pallas_call x1, Pallas kernels, local(): pl.pallas_call(first_kernel, out_shape=chunked, in_specs=[in_vmem(), in_v...  3.76 us
    pallas_call x1, Pallas kernels, local(): pl.pallas_call(second_kernel, out_shape=chunked, in_specs=[in_vmem(), in_...  3.63 us
    pallas_call x1, Pallas kernels, local(): pl.pallas_call(last_kernel, out_shape=jax.ShapeDtypeStruct((16, 8, 2, 8,...  2.27 us

profile of v1, /device:TPU:896, one launch (start us, length us, event | category | flops | bytes accessed | tf_op | source)
XLA Modules:
  0.0 80.8 jit_solution(5315409283954032777)
XLA Ops:
  0.0 3.8 %shard_map.37 = f32[32,64,128]{2,1,0:T(8,128)} custom-call(f32[2048,128]{1,0:T(8,128)} %bitcast.12, f32[4,2,128,128]{3,2,1,0:T(8,128)} %gates_ref.3, s32[3,128]{1,0:T(4,128)} %phase_smem.1, s32[3,128]{1,0:T(4,128)} %phase_smem.1), custom_call_target="tpu_custom_call" | custom-call | tf_op jit(solution)/shard_map/pallas_call | solution.py:141
  3.8 37.6 %all_to_all.10.x_ref = f32[32,64,128]{2,1,0:T(8,128)} all-to-all(f32[32,64,128]{2,1,0:T(8,128)} %shard_map.37), channel_id=1, replica_groups=mesh['top'=2,'rest'=32,'narrow'=16] {'top','narrow'}, dimensions={0} | all-to-all | bytes 2097152 | tf_op jit(solution)/shard_map/all_to_all | solution.py:152
  41.4 3.6 %shard_map.38 = f32[32,64,128]{2,1,0:T(8,128)} custom-call(f32[32,64,128]{2,1,0:T(8,128)} %all_to_all.10.x_ref, f32[4,2,128,128]{3,2,1,0:T(8,128)} %gates_ref.3), custom_call_target="tpu_custom_call" | custom-call | tf_op jit(solution)/shard_map/pallas_call | solution.py:153
  45.0 33.5 %all_to_all.11 = f32[32,64,128]{2,1,0:T(8,128)} all-to-all(f32[32,64,128]{2,1,0:T(8,128)} %shard_map.38), channel_id=1, replica_groups=mesh['top'=2,'rest'=32,'narrow'=16] {'top','narrow'}, dimensions={0} | all-to-all | bytes 2097152 | tf_op jit(solution)/shard_map/all_to_all | solution.py:159
  78.5 2.3 %shard_map.39 = f32[16,8,2,8,128]{4,3,2,1,0:T(8,128)} custom-call(f32[16,2,8,8,128]{4,3,2,1,0:T(8,128)} %bitcast.11), custom_call_target="tpu_custom_call" | custom-call | tf_op jit(solution)/shard_map/pallas_call | solution.py:160

commit v2 on v1

--- a/solution.py
+++ b/solution.py
@@ -9,9 +9,21 @@
 
 GATE = 128
 LANES = 128
+STAGGER_NS = 14000
+COPIES = 4
 GROUP = 32
+NARROW_BITS = ("n3", "n2", "n1", "n0")
+ORDER = ("top", "n3", "n2", "n1", "n0")
 
 angle_step = 2.0 * math.pi / 256.0
+
+
+def place(top, narrow):
+    bits = dict(zip(NARROW_BITS, (narrow >> 3, narrow >> 2 & 1, narrow >> 1 & 1, narrow & 1)), top=top)
+    index = 0
+    for name in ORDER:
+        index = index * 2 + bits[name]
+    return index
 
 
 def dot(a, b):
@@ -34,14 +46,38 @@
     return jnp.concatenate([upper, lower], axis=0)
 
 
-def first_kernel(x_ref, gates_ref, phase_ref, phase_smem, out_ref, phase_cols, mat_ref):
-    top = lax.axis_index("top") * 64 + lax.axis_index("rest") * 2 + lax.axis_index("narrow") // 8
-    top_phase = phase_smem[2, top]
+def first_kernel(
+    state_ref, gates_hbm, phase_hbm, out_ref, later_ref, phase_ref, phase_cols, mat_ref, gates_ref, x_ref, sems, row_sems
+):
+    phase_copy = pltpu.make_async_copy(phase_hbm, phase_ref, sems.at[2])
+    phase_copy.start()
+    gate_copy = pltpu.make_async_copy(gates_hbm.at[0:2], gates_ref, sems.at[0])
+    gate_copy.start()
+    height = x_ref.shape[0] // COPIES
+    row_copies = []
+    for part in range(COPIES):
+        rows = pl.ds(part * height, height)
+        row_copies.append(pltpu.make_async_copy(state_ref.at[rows], x_ref.at[rows], row_sems.at[part]))
+        row_copies[-1].start()
+    later_copy = pltpu.make_async_copy(gates_hbm.at[2:4], later_ref, sems.at[1])
+    later_copy.start()
+
+    if STAGGER_NS:
+
+        @pl.when(lax.axis_index("rest") % 2 == 1)
+        def _():
+            pl.delay(STAGGER_NS)
+
+    top = lax.axis_index("top") * 64 + lax.axis_index("rest") * 2 + lax.axis_index("n3")
+    phase_copy.wait()
+    lane_ids = lax.broadcasted_iota(jnp.int32, (1, LANES), 1)
+    top_phase = jnp.sum(jnp.where(lane_ids == top, phase_ref[2:3, :], 0), axis=1, keepdims=True)
     lane_angle = phase_ref[0:1, :].astype(jnp.float32) * angle_step
     row_angle = (phase_ref[1:2, :] + top_phase).astype(jnp.float32) * angle_step
     lane_cos, lane_sin = jnp.cos(lane_angle), jnp.sin(lane_angle)
     phase_cols[0] = jnp.broadcast_to(jnp.cos(row_angle), (GATE, LANES)).T
     phase_cols[1] = jnp.broadcast_to(jnp.sin(row_angle), (GATE, LANES)).T
+    gate_copy.wait()
 
     zero_re, zero_im = gates_ref[0, 0].T, gates_ref[0, 1].T
     turned_re = zero_re * lane_cos - zero_im * lane_sin
@@ -68,6 +104,8 @@
             mat_ref[at + 8 : at + 16, :LANES] = turned_im
             mat_ref[at + 8 : at + 16, LANES:] = turned_re
     left = split(mat_ref[...])
+    for copy in row_copies:
+        copy.wait()
 
     for pair in range(4):
         base = pair * 4 * GATE
@@ -85,17 +123,18 @@
         for half in range(2):
             block = pair * 2 + half
             out_ref[block * 4 : block * 4 + 4] = done[:, half * LANES : (half + 1) * LANES].reshape(4, 64, LANES)
+    later_copy.wait()
 
 
 def second_kernel(x_ref, gates_ref, out_ref):
-    third = split(real_form(gates_ref[2, 0], gates_ref[2, 1]))
-    fourth = split(real_form(gates_ref[3, 0], gates_ref[3, 1]))
+    third = split(real_form(gates_ref[0, 0], gates_ref[0, 1]))
+    fourth = split(real_form(gates_ref[1, 0], gates_ref[1, 1]))
     for quarter in range(4):
         row = quarter * 16
 
         def part(which, side):
             rows = slice(row + side * 8, row + side * 8 + 8)
-            return x_ref[which * 16 : which * 16 + 16, rows, :].reshape(GATE, LANES)
+            return jnp.concatenate([x_ref[place(which, narrow), rows, :] for narrow in range(16)], axis=0)
 
         gathered = jnp.concatenate(
             [jnp.concatenate([part(0, side), part(1, side)], axis=1) for side in range(2)], axis=0
@@ -120,56 +159,80 @@
                 for low in range(8):
                     for half in range(2):
                         at = side * 128 + which * 64 + low * 8
-                        out_ref[which * 16 + half * 8 + low, pl.ds(quarter * 2 + side, 8, stride=8), :] = done[
+                        out_ref[place(which, half * 8 + low), pl.ds(quarter * 2 + side, 8, stride=8), :] = done[
                             at : at + 8, half * LANES : (half + 1) * LANES
                         ]
 
 
-def last_kernel(x_ref, out_ref):
-    for bit in range(2):
-        out_ref[:, :, bit] = x_ref[:, bit]
+def last_kernel(x_ref, out_ref, sems):
+    copies = []
+    for part in range(4):
+        for bit in range(2):
+            blocks = pl.ds(part * 4, 4)
+            copies.append(
+                pltpu.make_async_copy(x_ref.at[blocks, bit], out_ref.at[blocks, :, bit], sems.at[part * 2 + bit])
+            )
+            copies[-1].start()
+    for copy in copies:
+        copy.wait()
 
 
 def in_vmem():
     return pl.BlockSpec(memory_space=pltpu.VMEM)
 
 
+def anywhere():
+    return pl.BlockSpec(memory_space=pl.ANY)
+
+
+def exchange(chunks):
+    return lax.all_to_all(chunks, ORDER, 0, 0, tiled=True)
+
+
 def local(state, gates, phase_index):
     local_amps = state.shape[1]
-    rows = state.reshape(2, local_amps // LANES, LANES).transpose(1, 0, 2).reshape(2 * local_amps // LANES, LANES)
-    chunked = jax.ShapeDtypeStruct((GROUP, 64, LANES), jnp.float32)
-    sent = pl.pallas_call(
+    row_count = local_amps // LANES
+    rows = state.reshape(2, row_count, LANES).transpose(1, 0, 2).reshape(2 * row_count, LANES)
+    chunked = pltpu.VMEM((GROUP, 64, LANES), jnp.float32)
+    half_gates = pltpu.VMEM((2, 2, GATE, GATE), jnp.float32)
+    sent, later_gates = pl.pallas_call(
         first_kernel,
-        out_shape=chunked,
-        in_specs=[in_vmem(), in_vmem(), in_vmem(), pl.BlockSpec(memory_space=pltpu.SMEM)],
-        out_specs=in_vmem(),
+        out_shape=[chunked, half_gates],
+        in_specs=[anywhere()] * 3,
+        out_specs=[in_vmem(), in_vmem()],
         scratch_shapes=[
+            pltpu.VMEM(phase_index.shape, jnp.int32),
             pltpu.VMEM((2, GATE, LANES), jnp.float32),
             pltpu.VMEM((2 * GATE, 2 * GATE), jnp.float32),
+            half_gates,
+            pltpu.VMEM((2 * row_count, LANES), jnp.float32),
+            pltpu.SemaphoreType.DMA((3,)),
+            pltpu.SemaphoreType.DMA((COPIES,)),
         ],
-    )(rows, gates, phase_index, phase_index)
-    group = ("top", "narrow")
-    held = lax.all_to_all(sent, group, 0, 0, tiled=True)
+    )(rows, gates, phase_index)
+    held = pltpu.with_memory_space_constraint(exchange(sent), pltpu.VMEM)
     back = pl.pallas_call(
         second_kernel,
         out_shape=chunked,
         in_specs=[in_vmem(), in_vmem()],
         out_specs=in_vmem(),
-    )(held, gates)
-    home = lax.all_to_all(back, group, 0, 0, tiled=True)
+    )(held, pltpu.with_memory_space_constraint(later_gates, pltpu.VMEM))
+    home = exchange(back).reshape(16, 2, 8, 8, LANES)
     ordered = pl.pallas_call(
         last_kernel,
         out_shape=jax.ShapeDtypeStruct((16, 8, 2, 8, LANES), jnp.float32),
         in_specs=[in_vmem()],
-        out_specs=in_vmem(),
-    )(home.reshape(16, 2, 8, 8, LANES))
-    return ordered.reshape(local_amps // LANES, 2, LANES).transpose(1, 0, 2).reshape(2, local_amps)
+        out_specs=anywhere(),
+        scratch_shapes=[pltpu.SemaphoreType.DMA((8,))],
+    )(pltpu.with_memory_space_constraint(home, pltpu.VMEM))
+    return ordered.reshape(row_count, 2, LANES).transpose(1, 0, 2).reshape(2, local_amps)
 
 
 def solution(mesh):
     wide, narrow = mesh.devices.shape
-    split_mesh = Mesh(mesh.devices.reshape(2, wide // 2, narrow), ("top", "rest", "narrow"))
-    amplitudes = P(None, ("top", "rest", "narrow"))
+    names = ("top", "rest") + NARROW_BITS
+    split_mesh = Mesh(mesh.devices.reshape(2, wide // 2, *([2] * (narrow.bit_length() - 1))), names)
+    amplitudes = P(None, names)
     return jax.shard_map(
         local, mesh=split_mesh, in_specs=(amplitudes, P(), P()), out_specs=amplitudes, check_vma=False
     )

time: 81.2 us -> 81.2 us (level)
  the two profiles are of different devices: /device:TPU:896 before, /device:TPU:1 now
where the time goes in v2:
time: 81.2 us; the launch traced here: 81 us
  blocking collectives  62.9 us (77%)
  Pallas kernels  18.1 us (22%)
    all_to_all x2, blocking collectives, exchange(): return lax.all_to_all(chunks, ORDER, 0, 0, tiled=True)  62.9 us
    pallas_call x1, Pallas kernels, local(): pl.pallas_call(first_kernel, out_shape=[chunked, half_gates], in_specs=[a...  15.7 us

profile of v2, /device:TPU:1, one launch (start us, length us, event | category | flops | bytes accessed | tf_op | source)
XLA Modules:
  0.0 81.0 jit_solution(16007656697147744876)
XLA Ops:
  0.0 15.7 %shard_map.37 = (f32[32,64,128]{2,1,0:T(8,128)S(1)}, f32[2,2,128,128]{3,2,1,0:T(8,128)S(1)}) custom-call(f32[2048,128]{1,0:T(8,128)} %bitcast.12, f32[4,2,128,128]{3,2,1,0:T(8,128)} %gates_hbm.1, s32[3,128]{1,0:T(4,128)} %phase_hbm.1), custom_call_target="tpu_custom_call" | custom-call | tf_op jit(solution)/shard_map/pallas_call | solution.py:198
  15.8 32.7 %all_to_all.10.x_ref = f32[32,64,128]{2,1,0:T(8,128)S(1)} all-to-all(f32[32,64,128]{2,1,0:T(8,128)S(1)} %get-tuple-element.7), channel_id=1, replica_groups=mesh['top'=2,'rest'=32,'n3'=2,'n2'=2,'n1'=2,'n0'=2] {'top','n3','n2','n1..., dimensions={0} | all-to-all | bytes 2097152 | tf_op jit(solution)/shard_map/all_to_all | solution.py:189
  48.5 1.3 %shard_map.38 = f32[32,64,128]{2,1,0:T(8,128)S(1)} custom-call(f32[32,64,128]{2,1,0:T(8,128)S(1)} %all_to_all.10.x_ref, f32[2,2,128,128]{3,2,1,0:T(8,128)S(1)} %get-tuple-element.8.gates_ref), custom_call_target="tpu_custom_call" | custom-call | tf_op jit(solution)/shard_map/pallas_call | solution.py:214
  49.8 30.2 %all_to_all.11 = f32[32,64,128]{2,1,0:T(8,128)S(1)} all-to-all(f32[32,64,128]{2,1,0:T(8,128)S(1)} %shard_map.38), channel_id=1, replica_groups=mesh['top'=2,'rest'=32,'n3'=2,'n2'=2,'n1'=2,'n0'=2] {'top','n3','n2','n1..., dimensions={0} | all-to-all | bytes 2097152 | tf_op jit(solution)/shard_map/all_to_all | solution.py:189
  80.0 1.0 %shard_map.39 = f32[16,8,2,8,128]{4,3,2,1,0:T(8,128)} custom-call(f32[16,2,8,8,128]{4,3,2,1,0:T(8,128)S(1)} %bitcast.11), custom_call_target="tpu_custom_call" | custom-call | tf_op jit(solution)/shard_map/pallas_call | solution.py:221

commit v3 on v2

--- a/solution.py
+++ b/solution.py
@@ -62,13 +62,13 @@
     later_copy = pltpu.make_async_copy(gates_hbm.at[2:4], later_ref, sems.at[1])
     later_copy.start()
 
-    if STAGGER_NS:
-
-        @pl.when(lax.axis_index("rest") % 2 == 1)
-        def _():
-            pl.delay(STAGGER_NS)
-
-    top = lax.axis_index("top") * 64 + lax.axis_index("rest") * 2 + lax.axis_index("n3")
+    rest = lax.axis_index("rest")
+
+    @pl.when((rest % 2 == 1) & (rest >= 2))
+    def _():
+        pl.delay(STAGGER_NS)
+
+    top = lax.axis_index("top") * 64 + rest * 2 + lax.axis_index("n3")
     phase_copy.wait()
     lane_ids = lax.broadcasted_iota(jnp.int32, (1, LANES), 1)
     top_phase = jnp.sum(jnp.where(lane_ids == top, phase_ref[2:3, :], 0), axis=1, keepdims=True)

time: 81.2 us -> 70.5 us (0.87)
  the two profiles are of different devices: /device:TPU:1 before, /device:TPU:16 now
where the time goes in v3:
time: 70.5 us; the launch traced here: 70.3 us
  blocking collectives  65.3 us (93%)
  Pallas kernels  4.97 us (7%)
    all_to_all x2, blocking collectives, exchange(): return lax.all_to_all(chunks, ORDER, 0, 0, tiled=True)  65.3 us
    pallas_call x1, Pallas kernels, local(): pl.pallas_call(first_kernel, out_shape=[chunked, half_gates], in_specs=[a...  2.64 us

profile of v3, /device:TPU:16, one launch (start us, length us, event | category | flops | bytes accessed | tf_op | source)
XLA Modules:
  0.0 70.3 jit_solution(15697078267086073062)
XLA Ops:
  0.0 2.6 %shard_map.37 = (f32[32,64,128]{2,1,0:T(8,128)S(1)}, f32[2,2,128,128]{3,2,1,0:T(8,128)S(1)}) custom-call(f32[2048,128]{1,0:T(8,128)} %bitcast.12, f32[4,2,128,128]{3,2,1,0:T(8,128)} %gates_hbm.1, s32[3,128]{1,0:T(4,128)} %phase_hbm.1), custom_call_target="tpu_custom_call" | custom-call | tf_op jit(solution)/shard_map/pallas_call | solution.py:198
  2.7 37.6 %all_to_all.10.x_ref = f32[32,64,128]{2,1,0:T(8,128)S(1)} all-to-all(f32[32,64,128]{2,1,0:T(8,128)S(1)} %get-tuple-element.7), channel_id=1, replica_groups=mesh['top'=2,'rest'=32,'n3'=2,'n2'=2,'n1'=2,'n0'=2] {'top','n3','n2','n1..., dimensions={0} | all-to-all | bytes 2097152 | tf_op jit(solution)/shard_map/all_to_all | solution.py:189
  40.3 1.3 %shard_map.38 = f32[32,64,128]{2,1,0:T(8,128)S(1)} custom-call(f32[32,64,128]{2,1,0:T(8,128)S(1)} %all_to_all.10.x_ref, f32[2,2,128,128]{3,2,1,0:T(8,128)S(1)} %get-tuple-element.8.gates_ref), custom_call_target="tpu_custom_call" | custom-call | tf_op jit(solution)/shard_map/pallas_call | solution.py:214
  41.6 27.7 %all_to_all.11 = f32[32,64,128]{2,1,0:T(8,128)S(1)} all-to-all(f32[32,64,128]{2,1,0:T(8,128)S(1)} %shard_map.38), channel_id=1, replica_groups=mesh['top'=2,'rest'=32,'n3'=2,'n2'=2,'n1'=2,'n0'=2] {'top','n3','n2','n1..., dimensions={0} | all-to-all | bytes 2097152 | tf_op jit(solution)/shard_map/all_to_all | solution.py:189
  69.3 1.0 %shard_map.39 = f32[16,8,2,8,128]{4,3,2,1,0:T(8,128)} custom-call(f32[16,2,8,8,128]{4,3,2,1,0:T(8,128)S(1)} %bitcast.11), custom_call_target="tpu_custom_call" | custom-call | tf_op jit(solution)/shard_map/pallas_call | solution.py:221

commit v4 on v3

--- a/solution.py
+++ b/solution.py
@@ -10,6 +10,7 @@
 GATE = 128
 LANES = 128
 STAGGER_NS = 14000
+FIRST_PLANE_NS = 3000
 COPIES = 4
 GROUP = 32
 NARROW_BITS = ("n3", "n2", "n1", "n0")
@@ -67,6 +68,10 @@
     @pl.when((rest % 2 == 1) & (rest >= 2))
     def _():
         pl.delay(STAGGER_NS)
+
+    @pl.when(rest == 0)
+    def _():
+        pl.delay(FIRST_PLANE_NS)
 
     top = lax.axis_index("top") * 64 + rest * 2 + lax.axis_index("n3")
     phase_copy.wait()

time: 70.5 us -> 69.3 us (0.983)
  blocking collectives: 65.3 us -> 62 us
  Pallas kernels: 4.97 us -> 7.07 us
    all_to_all x2, blocking collectives: 65.3 us -> 62 us  [exchange(): return lax.all_to_all(chunks, ORDER, 0, 0, tiled=True)]
    pallas_call x1, Pallas kernels: 2.64 us -> 4.74 us  [local(): pl.pallas_call(first_kernel, out_shape=[chunked, half_gates], in_specs=[a...]
where the time goes in v4:
time: 69.3 us; the launch traced here: 69.1 us
  blocking collectives  62 us (89%)
  Pallas kernels  7.07 us (10%)
    all_to_all x2, blocking collectives, exchange(): return lax.all_to_all(chunks, ORDER, 0, 0, tiled=True)  62 us
    pallas_call x1, Pallas kernels, local(): pl.pallas_call(first_kernel, out_shape=[chunked, half_gates], in_specs=[a...  4.74 us

profile of v4, /device:TPU:16, one launch (start us, length us, event | category | flops | bytes accessed | tf_op | source)
XLA Modules:
  0.0 69.1 jit_solution(16824042679514242573)
XLA Ops:
  0.0 4.7 %shard_map.37 = (f32[32,64,128]{2,1,0:T(8,128)S(1)}, f32[2,2,128,128]{3,2,1,0:T(8,128)S(1)}) custom-call(f32[2048,128]{1,0:T(8,128)} %bitcast.12, f32[4,2,128,128]{3,2,1,0:T(8,128)} %gates_hbm.1, s32[3,128]{1,0:T(4,128)} %phase_hbm.1), custom_call_target="tpu_custom_call" | custom-call | tf_op jit(solution)/shard_map/pallas_call | solution.py:203
  4.8 35.5 %all_to_all.10.x_ref = f32[32,64,128]{2,1,0:T(8,128)S(1)} all-to-all(f32[32,64,128]{2,1,0:T(8,128)S(1)} %get-tuple-element.7), channel_id=1, replica_groups=mesh['top'=2,'rest'=32,'n3'=2,'n2'=2,'n1'=2,'n0'=2] {'top','n3','n2','n1..., dimensions={0} | all-to-all | bytes 2097152 | tf_op jit(solution)/shard_map/all_to_all | solution.py:194
  40.3 1.3 %shard_map.38 = f32[32,64,128]{2,1,0:T(8,128)S(1)} custom-call(f32[32,64,128]{2,1,0:T(8,128)S(1)} %all_to_all.10.x_ref, f32[2,2,128,128]{3,2,1,0:T(8,128)S(1)} %get-tuple-element.8.gates_ref), custom_call_target="tpu_custom_call" | custom-call | tf_op jit(solution)/shard_map/pallas_call | solution.py:219
  41.6 26.5 %all_to_all.11 = f32[32,64,128]{2,1,0:T(8,128)S(1)} all-to-all(f32[32,64,128]{2,1,0:T(8,128)S(1)} %shard_map.38), channel_id=1, replica_groups=mesh['top'=2,'rest'=32,'n3'=2,'n2'=2,'n1'=2,'n0'=2] {'top','n3','n2','n1..., dimensions={0} | all-to-all | bytes 2097152 | tf_op jit(solution)/shard_map/all_to_all | solution.py:194
  68.1 1.0 %shard_map.39 = f32[16,8,2,8,128]{4,3,2,1,0:T(8,128)} custom-call(f32[16,2,8,8,128]{4,3,2,1,0:T(8,128)S(1)} %bitcast.11), custom_call_target="tpu_custom_call" | custom-call | tf_op jit(solution)/shard_map/pallas_call | solution.py:226

commit v5 on v4

--- a/solution.py
+++ b/solution.py
@@ -10,7 +10,7 @@
 GATE = 128
 LANES = 128
 STAGGER_NS = 14000
-FIRST_PLANE_NS = 3000
+FIRST_PLANE_NS = 4200
 COPIES = 4
 GROUP = 32
 NARROW_BITS = ("n3", "n2", "n1", "n0")
@@ -109,14 +109,14 @@
             mat_ref[at + 8 : at + 16, :LANES] = turned_im
             mat_ref[at + 8 : at + 16, LANES:] = turned_re
     left = split(mat_ref[...])
-    for copy in row_copies:
-        copy.wait()
-
-    for pair in range(4):
+
+    def stage_one(pair):
         base = pair * 4 * GATE
         real = x_ref[pl.ds(base, 2 * GATE, stride=2), :]
         imag = x_ref[pl.ds(base + 1, 2 * GATE, stride=2), :]
-        moved = product(split(jnp.concatenate([real, imag], axis=1)), right)
+        return product(split(jnp.concatenate([real, imag], axis=1)), right)
+
+    def stage_two(pair, moved):
         turned = jnp.concatenate(
             [
                 jnp.concatenate([moved[:GATE, :LANES], moved[GATE:, :LANES]], axis=1),
@@ -128,24 +128,29 @@
         for half in range(2):
             block = pair * 2 + half
             out_ref[block * 4 : block * 4 + 4] = done[:, half * LANES : (half + 1) * LANES].reshape(4, 64, LANES)
+
+    for copy in row_copies:
+        copy.wait()
+    moved = [stage_one(pair) for pair in range(4)]
+    for pair in range(4):
+        stage_two(pair, moved[pair])
     later_copy.wait()
 
 
 def second_kernel(x_ref, gates_ref, out_ref):
     third = split(real_form(gates_ref[0, 0], gates_ref[0, 1]))
     fourth = split(real_form(gates_ref[1, 0], gates_ref[1, 1]))
-    for quarter in range(4):
-        row = quarter * 16
-
+    def stage_one(quarter):
         def part(which, side):
-            rows = slice(row + side * 8, row + side * 8 + 8)
+            rows = slice(quarter * 16 + side * 8, quarter * 16 + side * 8 + 8)
             return jnp.concatenate([x_ref[place(which, narrow), rows, :] for narrow in range(16)], axis=0)
 
         gathered = jnp.concatenate(
             [jnp.concatenate([part(0, side), part(1, side)], axis=1) for side in range(2)], axis=0
         )
-        moved = product(third, split(gathered))
-
+        return product(third, split(gathered))
+
+    def stage_two(quarter, moved):
         def piece(side, which, half):
             at = side * GATE + half * 64
             return moved[at : at + 64, which * LANES : (which + 1) * LANES]
@@ -167,6 +172,10 @@
                         out_ref[place(which, half * 8 + low), pl.ds(quarter * 2 + side, 8, stride=8), :] = done[
                             at : at + 8, half * LANES : (half + 1) * LANES
                         ]
+
+    moved = [stage_one(quarter) for quarter in range(4)]
+    for quarter in range(4):
+        stage_two(quarter, moved[quarter])
 
 
 def last_kernel(x_ref, out_ref, sems):

time: 69.3 us -> 67.3 us (0.971)
  the two profiles are of different devices: /device:TPU:16 before, /device:TPU:129 now
where the time goes in v5:
time: 67.3 us; the launch traced here: 67.1 us
  blocking collectives  49.6 us (74%)
  Pallas kernels  17.5 us (26%)
    all_to_all x2, blocking collectives, exchange(): return lax.all_to_all(chunks, ORDER, 0, 0, tiled=True)  49.6 us
    pallas_call x1, Pallas kernels, local(): pl.pallas_call(first_kernel, out_shape=[chunked, half_gates], in_specs=[a...  15.4 us

profile of v5, /device:TPU:129, one launch (start us, length us, event | category | flops | bytes accessed | tf_op | source)
XLA Modules:
  0.0 67.1 jit_solution(15114665831625987461)
XLA Ops:
  0.0 15.4 %shard_map.37 = (f32[32,64,128]{2,1,0:T(8,128)S(1)}, f32[2,2,128,128]{3,2,1,0:T(8,128)S(1)}) custom-call(f32[2048,128]{1,0:T(8,128)} %bitcast.12, f32[4,2,128,128]{3,2,1,0:T(8,128)} %gates_hbm.1, s32[3,128]{1,0:T(4,128)} %phase_hbm.1), custom_call_target="tpu_custom_call" | custom-call | tf_op jit(solution)/shard_map/pallas_call | solution.py:212
  15.4 27.2 %all_to_all.10.x_ref = f32[32,64,128]{2,1,0:T(8,128)S(1)} all-to-all(f32[32,64,128]{2,1,0:T(8,128)S(1)} %get-tuple-element.7), channel_id=1, replica_groups=mesh['top'=2,'rest'=32,'n3'=2,'n2'=2,'n1'=2,'n0'=2] {'top','n3','n2','n1..., dimensions={0} | all-to-all | bytes 2097152 | tf_op jit(solution)/shard_map/all_to_all | solution.py:203
  42.6 1.0 %shard_map.38 = f32[32,64,128]{2,1,0:T(8,128)S(1)} custom-call(f32[32,64,128]{2,1,0:T(8,128)S(1)} %all_to_all.10.x_ref, f32[2,2,128,128]{3,2,1,0:T(8,128)S(1)} %get-tuple-element.8.gates_ref), custom_call_target="tpu_custom_call" | custom-call | tf_op jit(solution)/shard_map/pallas_call | solution.py:228
  43.7 22.4 %all_to_all.11 = f32[32,64,128]{2,1,0:T(8,128)S(1)} all-to-all(f32[32,64,128]{2,1,0:T(8,128)S(1)} %shard_map.38), channel_id=1, replica_groups=mesh['top'=2,'rest'=32,'n3'=2,'n2'=2,'n1'=2,'n0'=2] {'top','n3','n2','n1..., dimensions={0} | all-to-all | bytes 2097152 | tf_op jit(solution)/shard_map/all_to_all | solution.py:203
  66.0 1.0 %shard_map.39 = f32[16,8,2,8,128]{4,3,2,1,0:T(8,128)} custom-call(f32[16,2,8,8,128]{4,3,2,1,0:T(8,128)S(1)} %bitcast.11), custom_call_target="tpu_custom_call" | custom-call | tf_op jit(solution)/shard_map/pallas_call | solution.py:235

commit v6 on v5

--- a/solution.py
+++ b/solution.py
@@ -9,7 +9,7 @@
 
 GATE = 128
 LANES = 128
-STAGGER_NS = 14000
+STAGGER_NS = 10800
 FIRST_PLANE_NS = 4200
 COPIES = 4
 GROUP = 32
@@ -65,7 +65,7 @@
 
     rest = lax.axis_index("rest")
 
-    @pl.when((rest % 2 == 1) & (rest >= 2))
+    @pl.when((rest % 2 == 0) & (rest >= 2))
     def _():
         pl.delay(STAGGER_NS)
 

time: 67.3 us -> 66.3 us (0.985)
  the two profiles are of different devices: /device:TPU:129 before, /device:TPU:16 now
where the time goes in v6:
time: 66.3 us; the launch traced here: 66.1 us
  blocking collectives  58.4 us (88%)
  Pallas kernels  7.69 us (12%)
    all_to_all x2, blocking collectives, exchange(): return lax.all_to_all(chunks, ORDER, 0, 0, tiled=True)  58.4 us
    pallas_call x1, Pallas kernels, local(): pl.pallas_call(first_kernel, out_shape=[chunked, half_gates], in_specs=[a...  5.63 us

profile of v6, /device:TPU:16, one launch (start us, length us, event | category | flops | bytes accessed | tf_op | source)
XLA Modules:
  0.0 66.1 jit_solution(18253795818450615481)
XLA Ops:
  0.0 5.6 %shard_map.37 = (f32[32,64,128]{2,1,0:T(8,128)S(1)}, f32[2,2,128,128]{3,2,1,0:T(8,128)S(1)}) custom-call(f32[2048,128]{1,0:T(8,128)} %bitcast.12, f32[4,2,128,128]{3,2,1,0:T(8,128)} %gates_hbm.1, s32[3,128]{1,0:T(4,128)} %phase_hbm.1), custom_call_target="tpu_custom_call" | custom-call | tf_op jit(solution)/shard_map/pallas_call | solution.py:212
  5.6 34.3 %all_to_all.10.x_ref = f32[32,64,128]{2,1,0:T(8,128)S(1)} all-to-all(f32[32,64,128]{2,1,0:T(8,128)S(1)} %get-tuple-element.7), channel_id=1, replica_groups=mesh['top'=2,'rest'=32,'n3'=2,'n2'=2,'n1'=2,'n0'=2] {'top','n3','n2','n1..., dimensions={0} | all-to-all | bytes 2097152 | tf_op jit(solution)/shard_map/all_to_all | solution.py:203
  39.9 1.0 %shard_map.38 = f32[32,64,128]{2,1,0:T(8,128)S(1)} custom-call(f32[32,64,128]{2,1,0:T(8,128)S(1)} %all_to_all.10.x_ref, f32[2,2,128,128]{3,2,1,0:T(8,128)S(1)} %get-tuple-element.8.gates_ref), custom_call_target="tpu_custom_call" | custom-call | tf_op jit(solution)/shard_map/pallas_call | solution.py:228
  41.0 24.1 %all_to_all.11 = f32[32,64,128]{2,1,0:T(8,128)S(1)} all-to-all(f32[32,64,128]{2,1,0:T(8,128)S(1)} %shard_map.38), channel_id=1, replica_groups=mesh['top'=2,'rest'=32,'n3'=2,'n2'=2,'n1'=2,'n0'=2] {'top','n3','n2','n1..., dimensions={0} | all-to-all | bytes 2097152 | tf_op jit(solution)/shard_map/all_to_all | solution.py:203
  65.0 1.0 %shard_map.39 = f32[16,8,2,8,128]{4,3,2,1,0:T(8,128)} custom-call(f32[16,2,8,8,128]{4,3,2,1,0:T(8,128)S(1)} %bitcast.11), custom_call_target="tpu_custom_call" | custom-call | tf_op jit(solution)/shard_map/pallas_call | solution.py:235

commit v7 on v6

--- a/solution.py
+++ b/solution.py
@@ -9,8 +9,8 @@
 
 GATE = 128
 LANES = 128
-STAGGER_NS = 10800
-FIRST_PLANE_NS = 4200
+STAGGER_NS = 10400
+FIRST_PLANE_NS = 3800
 COPIES = 4
 GROUP = 32
 NARROW_BITS = ("n3", "n2", "n1", "n0")
@@ -47,8 +47,18 @@
     return jnp.concatenate([upper, lower], axis=0)
 
 
+def blocks_swapped(value):
+    return jnp.concatenate(
+        [
+            jnp.concatenate([value[:GATE, column : column + LANES], value[GATE:, column : column + LANES]], axis=1)
+            for column in (0, LANES)
+        ],
+        axis=0,
+    )
+
+
 def first_kernel(
-    state_ref, gates_hbm, phase_hbm, out_ref, later_ref, phase_ref, phase_cols, mat_ref, gates_ref, x_ref, sems, row_sems
+    state_ref, gates_hbm, phase_hbm, out_ref, later_ref, turn_ref, phase_ref, phase_cols, mat_ref, gates_ref, x_ref, sems, row_sems
 ):
     phase_copy = pltpu.make_async_copy(phase_hbm, phase_ref, sems.at[2])
     phase_copy.start()
@@ -87,14 +97,12 @@
     zero_re, zero_im = gates_ref[0, 0].T, gates_ref[0, 1].T
     turned_re = zero_re * lane_cos - zero_im * lane_sin
     turned_im = zero_re * lane_sin + zero_im * lane_cos
-    right = split(
-        jnp.concatenate(
-            [
-                jnp.concatenate([turned_re, turned_im], axis=1),
-                jnp.concatenate([-turned_im, turned_re], axis=1),
-            ],
-            axis=0,
-        )
+    turn_ref[...] = jnp.concatenate(
+        [
+            jnp.concatenate([turned_re, turned_im], axis=1),
+            jnp.concatenate([-turned_im, turned_re], axis=1),
+        ],
+        axis=0,
     )
     for high in range(2):
         for low in range(8):
@@ -110,45 +118,51 @@
             mat_ref[at + 8 : at + 16, LANES:] = turned_re
     left = split(mat_ref[...])
 
-    def stage_one(pair):
+    def rows_of(pair):
         base = pair * 4 * GATE
-        real = x_ref[pl.ds(base, 2 * GATE, stride=2), :]
-        imag = x_ref[pl.ds(base + 1, 2 * GATE, stride=2), :]
-        return product(split(jnp.concatenate([real, imag], axis=1)), right)
-
-    def stage_two(pair, moved):
-        turned = jnp.concatenate(
+        return jnp.concatenate(
+            [x_ref[pl.ds(base + part, 2 * GATE, stride=2), :] for part in range(2)], axis=1
+        )
+
+    def finish(pair, moved):
+        done = product(left, split(blocks_swapped(moved)))
+        for half in range(2):
+            block = pair * 2 + half
+            out_ref[block * 4 : block * 4 + 4] = done[:, half * LANES : (half + 1) * LANES].reshape(4, 64, LANES)
+
+    for copy in row_copies:
+        copy.wait()
+
+    @pl.when(rest % 2 == 1)
+    def _():
+        for pair in range(4):
+            finish(pair, rows_of(pair))
+
+    @pl.when(rest % 2 == 0)
+    def _():
+        right = split(turn_ref[...])
+        moved = [product(split(rows_of(pair)), right) for pair in range(4)]
+        for pair in range(4):
+            finish(pair, moved[pair])
+
+    later_copy.wait()
+
+
+def second_kernel(x_ref, gates_ref, turn_ref, out_ref):
+    third = split(real_form(gates_ref[0, 0], gates_ref[0, 1]))
+    fourth = split(real_form(gates_ref[1, 0], gates_ref[1, 1]))
+    def gathered(quarter, by_part):
+        def block(which, side):
+            rows = slice(quarter * 16 + side * 8, quarter * 16 + side * 8 + 8)
+            return jnp.concatenate([x_ref[place(which, narrow), rows, :] for narrow in range(16)], axis=0)
+
+        return jnp.concatenate(
             [
-                jnp.concatenate([moved[:GATE, :LANES], moved[GATE:, :LANES]], axis=1),
-                jnp.concatenate([moved[:GATE, LANES:], moved[GATE:, LANES:]], axis=1),
+                jnp.concatenate([block(other, outer) if by_part else block(outer, other) for other in range(2)], axis=1)
+                for outer in range(2)
             ],
             axis=0,
         )
-        done = product(left, split(turned))
-        for half in range(2):
-            block = pair * 2 + half
-            out_ref[block * 4 : block * 4 + 4] = done[:, half * LANES : (half + 1) * LANES].reshape(4, 64, LANES)
-
-    for copy in row_copies:
-        copy.wait()
-    moved = [stage_one(pair) for pair in range(4)]
-    for pair in range(4):
-        stage_two(pair, moved[pair])
-    later_copy.wait()
-
-
-def second_kernel(x_ref, gates_ref, out_ref):
-    third = split(real_form(gates_ref[0, 0], gates_ref[0, 1]))
-    fourth = split(real_form(gates_ref[1, 0], gates_ref[1, 1]))
-    def stage_one(quarter):
-        def part(which, side):
-            rows = slice(quarter * 16 + side * 8, quarter * 16 + side * 8 + 8)
-            return jnp.concatenate([x_ref[place(which, narrow), rows, :] for narrow in range(16)], axis=0)
-
-        gathered = jnp.concatenate(
-            [jnp.concatenate([part(0, side), part(1, side)], axis=1) for side in range(2)], axis=0
-        )
-        return product(third, split(gathered))
 
     def stage_two(quarter, moved):
         def piece(side, which, half):
@@ -173,9 +187,21 @@
                             at : at + 8, half * LANES : (half + 1) * LANES
                         ]
 
-    moved = [stage_one(quarter) for quarter in range(4)]
-    for quarter in range(4):
-        stage_two(quarter, moved[quarter])
+    rest = lax.axis_index("rest")
+
+    @pl.when(rest % 2 == 1)
+    def _():
+        right = split(turn_ref[...])
+        turned = [product(split(gathered(quarter, False)), right) for quarter in range(4)]
+        moved = [product(third, split(blocks_swapped(turned[quarter]))) for quarter in range(4)]
+        for quarter in range(4):
+            stage_two(quarter, moved[quarter])
+
+    @pl.when(rest % 2 == 0)
+    def _():
+        moved = [product(third, split(gathered(quarter, True))) for quarter in range(4)]
+        for quarter in range(4):
+            stage_two(quarter, moved[quarter])
 
 
 def last_kernel(x_ref, out_ref, sems):
@@ -209,11 +235,12 @@
     rows = state.reshape(2, row_count, LANES).transpose(1, 0, 2).reshape(2 * row_count, LANES)
     chunked = pltpu.VMEM((GROUP, 64, LANES), jnp.float32)
     half_gates = pltpu.VMEM((2, 2, GATE, GATE), jnp.float32)
-    sent, later_gates = pl.pallas_call(
+    turn = pltpu.VMEM((2 * GATE, 2 * GATE), jnp.float32)
+    sent, later_gates, lane_gate = pl.pallas_call(
         first_kernel,
-        out_shape=[chunked, half_gates],
+        out_shape=[chunked, half_gates, turn],
         in_specs=[anywhere()] * 3,
-        out_specs=[in_vmem(), in_vmem()],
+        out_specs=[in_vmem()] * 3,
         scratch_shapes=[
             pltpu.VMEM(phase_index.shape, jnp.int32),
             pltpu.VMEM((2, GATE, LANES), jnp.float32),
@@ -228,9 +255,13 @@
     back = pl.pallas_call(
         second_kernel,
         out_shape=chunked,
-        in_specs=[in_vmem(), in_vmem()],
+        in_specs=[in_vmem()] * 3,
         out_specs=in_vmem(),
-    )(held, pltpu.with_memory_space_constraint(later_gates, pltpu.VMEM))
+    )(
+        held,
+        pltpu.with_memory_space_constraint(later_gates, pltpu.VMEM),
+        pltpu.with_memory_space_constraint(lane_gate, pltpu.VMEM),
+    )
     home = exchange(back).reshape(16, 2, 8, 8, LANES)
     ordered = pl.pallas_call(
         last_kernel,

time: 66.3 us -> 66.3 us (level)
  no operation moved by 1% of the time
where the time goes in v7:
time: 66.3 us; the launch traced here: 66.1 us
  blocking collectives  58.8 us (89%)
  Pallas kernels  7.34 us (11%)
    all_to_all x2, blocking collectives, exchange(): return lax.all_to_all(chunks, ORDER, 0, 0, tiled=True)  58.8 us
    pallas_call x1, Pallas kernels, local(): pl.pallas_call(first_kernel, out_shape=[chunked, half_gates, turn], in_sp...  5.22 us

profile of v7, /device:TPU:16, one launch (start us, length us, event | category | flops | bytes accessed | tf_op | source)
XLA Modules:
  0.0 66.1 jit_solution(10826683015441063941)
XLA Ops:
  0.0 5.2 %shard_map.37 = (f32[32,64,128]{2,1,0:T(8,128)S(1)}, f32[2,2,128,128]{3,2,1,0:T(8,128)S(1)}, f32[256,256]{1,0:T(8,128)S(1)}) custom-call(f32[2048,128]{1,0:T(8,128)} %bitcast.12, f32[4,2,128,128]{3,2,1,0:T(8,128)} %gates_hbm.1, s32[3,128]{1,0:T(4,128)} %phase_hbm.1), custom_call_target="tpu_custom_call" | custom-call | tf_op jit(solution)/shard_map/pallas_call | solution.py:239
  5.2 34.3 %all_to_all.10.x_ref = f32[32,64,128]{2,1,0:T(8,128)S(1)} all-to-all(f32[32,64,128]{2,1,0:T(8,128)S(1)} %get-tuple-element.8), channel_id=1, replica_groups=mesh['top'=2,'rest'=32,'n3'=2,'n2'=2,'n1'=2,'n0'=2] {'top','n3','n2','n1..., dimensions={0} | all-to-all | bytes 2097152 | tf_op jit(solution)/shard_map/all_to_all | solution.py:229
  39.5 1.1 %shard_map.38 = f32[32,64,128]{2,1,0:T(8,128)S(1)} custom-call(f32[32,64,128]{2,1,0:T(8,128)S(1)} %all_to_all.10.x_ref, f32[2,2,128,128]{3,2,1,0:T(8,128)S(1)} %get-tuple-element.9.gates_ref, f32[256,256]{1,0:T(8,128)S(1)} %get-tuple-element.10.turn_ref), custom_call_target="tpu_custom_call" | custom-call | tf_op jit(solution)/shard_map/pallas_call | solution.py:255
  40.7 24.5 %all_to_all.11 = f32[32,64,128]{2,1,0:T(8,128)S(1)} all-to-all(f32[32,64,128]{2,1,0:T(8,128)S(1)} %shard_map.38), channel_id=1, replica_groups=mesh['top'=2,'rest'=32,'n3'=2,'n2'=2,'n1'=2,'n0'=2] {'top','n3','n2','n1..., dimensions={0} | all-to-all | bytes 2097152 | tf_op jit(solution)/shard_map/all_to_all | solution.py:229
  65.1 1.0 %shard_map.39 = f32[16,8,2,8,128]{4,3,2,1,0:T(8,128)} custom-call(f32[16,2,8,8,128]{4,3,2,1,0:T(8,128)S(1)} %bitcast.11), custom_call_target="tpu_custom_call" | custom-call | tf_op jit(solution)/shard_map/pallas_call | solution.py:266

commit v8 on v7

--- a/solution.py
+++ b/solution.py
@@ -9,8 +9,8 @@
 
 GATE = 128
 LANES = 128
-STAGGER_NS = 10400
-FIRST_PLANE_NS = 3800
+STAGGER_NS = 10200
+FIRST_PLANE_NS = 3300
 COPIES = 4
 GROUP = 32
 NARROW_BITS = ("n3", "n2", "n1", "n0")
@@ -58,7 +58,8 @@
 
 
 def first_kernel(
-    state_ref, gates_hbm, phase_hbm, out_ref, later_ref, turn_ref, phase_ref, phase_cols, mat_ref, gates_ref, x_ref, sems, row_sems
+    state_ref, gates_hbm, phase_hbm, out_ref, later_ref, turn_ref, ready_ref, phase_ref, phase_cols, mat_ref, gates_ref, x_ref,
+    sems, row_sems
 ):
     phase_copy = pltpu.make_async_copy(phase_hbm, phase_ref, sems.at[2])
     phase_copy.start()
@@ -137,20 +138,20 @@
     def _():
         for pair in range(4):
             finish(pair, rows_of(pair))
+        later_copy.wait()
 
     @pl.when(rest % 2 == 0)
     def _():
+        later_copy.wait()
+        for gate in range(2):
+            ready_ref[gate, 0], ready_ref[gate, 1] = split(real_form(later_ref[gate, 0], later_ref[gate, 1]))
         right = split(turn_ref[...])
         moved = [product(split(rows_of(pair)), right) for pair in range(4)]
         for pair in range(4):
             finish(pair, moved[pair])
 
-    later_copy.wait()
-
-
-def second_kernel(x_ref, gates_ref, turn_ref, out_ref):
-    third = split(real_form(gates_ref[0, 0], gates_ref[0, 1]))
-    fourth = split(real_form(gates_ref[1, 0], gates_ref[1, 1]))
+
+def second_kernel(x_ref, gates_ref, turn_ref, ready_ref, out_ref):
     def gathered(quarter, by_part):
         def block(which, side):
             rows = slice(quarter * 16 + side * 8, quarter * 16 + side * 8 + 8)
@@ -164,7 +165,7 @@
             axis=0,
         )
 
-    def stage_two(quarter, moved):
+    def stage_two(quarter, moved, fourth):
         def piece(side, which, half):
             at = side * GATE + half * 64
             return moved[at : at + 64, which * LANES : (which + 1) * LANES]
@@ -191,17 +192,19 @@
 
     @pl.when(rest % 2 == 1)
     def _():
+        third, fourth = (split(real_form(gates_ref[gate, 0], gates_ref[gate, 1])) for gate in range(2))
         right = split(turn_ref[...])
         turned = [product(split(gathered(quarter, False)), right) for quarter in range(4)]
         moved = [product(third, split(blocks_swapped(turned[quarter]))) for quarter in range(4)]
         for quarter in range(4):
-            stage_two(quarter, moved[quarter])
+            stage_two(quarter, moved[quarter], fourth)
 
     @pl.when(rest % 2 == 0)
     def _():
+        third, fourth = ((ready_ref[gate, 0], ready_ref[gate, 1]) for gate in range(2))
         moved = [product(third, split(gathered(quarter, True))) for quarter in range(4)]
         for quarter in range(4):
-            stage_two(quarter, moved[quarter])
+            stage_two(quarter, moved[quarter], fourth)
 
 
 def last_kernel(x_ref, out_ref, sems):
@@ -236,11 +239,12 @@
     chunked = pltpu.VMEM((GROUP, 64, LANES), jnp.float32)
     half_gates = pltpu.VMEM((2, 2, GATE, GATE), jnp.float32)
     turn = pltpu.VMEM((2 * GATE, 2 * GATE), jnp.float32)
-    sent, later_gates, lane_gate = pl.pallas_call(
+    ready = pltpu.VMEM((2, 2, 2 * GATE, 2 * GATE), jnp.bfloat16)
+    sent, later_gates, lane_gate, ready_gates = pl.pallas_call(
         first_kernel,
-        out_shape=[chunked, half_gates, turn],
+        out_shape=[chunked, half_gates, turn, ready],
         in_specs=[anywhere()] * 3,
-        out_specs=[in_vmem()] * 3,
+        out_specs=[in_vmem()] * 4,
         scratch_shapes=[
             pltpu.VMEM(phase_index.shape, jnp.int32),
             pltpu.VMEM((2, GATE, LANES), jnp.float32),
@@ -255,12 +259,13 @@
     back = pl.pallas_call(
         second_kernel,
         out_shape=chunked,
-        in_specs=[in_vmem()] * 3,
+        in_specs=[in_vmem()] * 4,
         out_specs=in_vmem(),
     )(
         held,
         pltpu.with_memory_space_constraint(later_gates, pltpu.VMEM),
         pltpu.with_memory_space_constraint(lane_gate, pltpu.VMEM),
+        pltpu.with_memory_space_constraint(ready_gates, pltpu.VMEM),
     )
     home = exchange(back).reshape(16, 2, 8, 8, LANES)
     ordered = pl.pallas_call(

time: 66.3 us -> 71.3 us (1.075)
  local copies, waits for them, and re-layouts: 0 us -> 3.47 us
  blocking collectives: 58.8 us -> 60.6 us
    unnamed x0 -> x8, local copies, waits for them, and re-layouts: none -> 3.47 us
    all_to_all x2, blocking collectives: 58.8 us -> 60.6 us  [exchange(): return lax.all_to_all(chunks, ORDER, 0, 0, tiled=True)]
where the time goes in v8:
time: 71.3 us; the launch traced here: 71 us
  blocking collectives  60.6 us (85%)
  Pallas kernels  6.88 us (10%)
  local copies, waits for them, and re-layouts  3.47 us (5%)
    all_to_all x2, blocking collectives, exchange(): return lax.all_to_all(chunks, ORDER, 0, 0, tiled=True)  60.6 us
    pallas_call x1, Pallas kernels, local(): pl.pallas_call(first_kernel, out_shape=[chunked, half_gates, turn, ready]...  4.81 us
    unnamed x8, local copies, waits for them, and re-layouts  3.47 us

profile of v8, /device:TPU:16, one launch (start us, length us, event | category | flops | bytes accessed | tf_op | source)
XLA Modules:
  0.0 71.0 jit_solution(2772782234973225693)
XLA Ops:
  0.0 4.8 %shard_map.37 = (f32[32,64,128]{2,1,0:T(8,128)S(1)}, f32[2,2,128,128]{3,2,1,0:T(8,128)S(1)}, f32[256,256]{1,0:T(8,128)S(1)}, bf16[2,2,256,256]{3,2,1,0:T(8,128)(2,1)S(1)}) custom-call(f32[2048,128]{1,0:T(8,128)} %bitcast.12, f32[4,2,128,128]{3,2,1,0:T(8,128)} %gates_hbm.1, s32[3,128]{1,0:T(4,128)} %phase_hbm.1), custom_call_target="tpu_custom_call" | custom-call | tf_op jit(solution)/shard_map/pallas_call | solution.py:243
  4.8 0.0 copy-start
  4.8 0.8 %copy-done = bf16[2,2,256,256]{3,2,1,0:T(8,128)(2,1)} copy-done((bf16[2,2,256,256]{3,2,1,0:T(8,128)(2,1)}, bf16[2,2,256,256]{3,2,1,0:T(8,128)(2,1)S(1)}, u32[]{:S(2)}) %copy-start) | copy-done | bytes 524312
  5.6 0.0 copy-start.2
  5.6 0.7 copy-done.2
  6.3 34.7 %all_to_all.10.x_ref = f32[32,64,128]{2,1,0:T(8,128)S(1)} all-to-all(f32[32,64,128]{2,1,0:T(8,128)S(1)} %get-tuple-element.9), channel_id=1, replica_groups=mesh['top'=2,'rest'=32,'n3'=2,'n2'=2,'n1'=2,'n0'=2] {'top','n3','n2','n1..., dimensions={0} | all-to-all | bytes 2097152 | tf_op jit(solution)/shard_map/all_to_all | solution.py:232
  41.0 0.0 copy-start.1
  41.0 1.0 %copy-done.1 = bf16[2,2,256,256]{3,2,1,0:T(8,128)(2,1)S(1)} copy-done((bf16[2,2,256,256]{3,2,1,0:T(8,128)(2,1)S(1)}, bf16[2,2,256,256]{3,2,1,0:T(8,128)(2,1)}, u32[]{:S(2)}) %copy-start.1) | copy-done | bytes 524312
  42.1 0.0 copy-start.3
  42.1 0.9 %copy-done.3 = f32[256,256]{1,0:T(8,128)S(1)} copy-done((f32[256,256]{1,0:T(8,128)S(1)}, f32[256,256]{1,0:T(8,128)}, u32[]{:S(2)}) %copy-start.3) | copy-done | bytes 262168
  43.0 1.0 %shard_map.38 = f32[32,64,128]{2,1,0:T(8,128)S(1)} custom-call(f32[32,64,128]{2,1,0:T(8,128)S(1)} %all_to_all.10.x_ref, f32[2,2,128,128]{3,2,1,0:T(8,128)S(1)} %get-tuple-element.10.gates_ref, f32[256,256]{1,0:T(8,128)S(1)} %copy-done.3, bf16[2,2,256,256]{3,2,1,0:T(8,128)(2,1)S(1)} %copy-done.1), custom_call_target="tpu_custom_call" | custom-call | tf_op jit(solution)/shard_map/pallas_call | solution.py:259
  44.1 25.9 %all_to_all.11 = f32[32,64,128]{2,1,0:T(8,128)S(1)} all-to-all(f32[32,64,128]{2,1,0:T(8,128)S(1)} %shard_map.38), channel_id=1, replica_groups=mesh['top'=2,'rest'=32,'n3'=2,'n2'=2,'n1'=2,'n0'=2] {'top','n3','n2','n1..., dimensions={0} | all-to-all | bytes 2097152 | tf_op jit(solution)/shard_map/all_to_all | solution.py:232
  70.0 1.0 %shard_map.39 = f32[16,8,2,8,128]{4,3,2,1,0:T(8,128)} custom-call(f32[16,2,8,8,128]{4,3,2,1,0:T(8,128)S(1)} %bitcast.11), custom_call_target="tpu_custom_call" | custom-call | tf_op jit(solution)/shard_map/pallas_call | solution.py:271
Async XLA Ops:
  4.8 0.8 %copy-start = (bf16[2,2,256,256]{3,2,1,0:T(8,128)(2,1)}, bf16[2,2,256,256]{3,2,1,0:T(8,128)(2,1)S(1)}, u32[]{:S(2)}) copy-start(bf16[2,2,256,256]{3,2,1,0:T(8,128)(2,1)S(1)} %get-tuple-element.12.ready_ref) | copy-start | bytes 1572868
  5.6 0.7 copy-start.2
  41.0 1.0 %copy-start.1 = (bf16[2,2,256,256]{3,2,1,0:T(8,128)(2,1)S(1)}, bf16[2,2,256,256]{3,2,1,0:T(8,128)(2,1)}, u32[]{:S(2)}) copy-start(bf16[2,2,256,256]{3,2,1,0:T(8,128)(2,1)} %copy-done) | copy-start | bytes 1572868
  42.1 0.9 %copy-start.3 = (f32[256,256]{1,0:T(8,128)S(1)}, f32[256,256]{1,0:T(8,128)}, u32[]{:S(2)}) copy-start(f32[256,256]{1,0:T(8,128)} %copy-done.2) | copy-start | bytes 786436
